TPU v7x, 32 devices: a whole 2x2x4 slice. The times are simulated.
32 devices in a mesh: expert: 8 (over z, x), dp: 4 (over y, core).
Axes of the slice: x: 2, y: 2, z: 4, core: 2. Of those that a mesh axis runs over, the one named last changes fastest.
Arguments:
- enc_state: bfloat16 [4, 8, 256, 1024], P('dp', 'expert'), may hold values from -6 to 6
- baseline: bfloat16 [4, 8, 256, 1024], P('dp', 'expert'), may hold values from -6 to 6
- enc_keys: bfloat16 [4, 8, 256, 1024], P('dp', 'expert'), may hold values from -4 to 4
- dec_queries: bfloat16 [4, 8, 128, 1024], P('dp', 'expert'), may hold values from -200 to 200
- out_mult: bfloat16 [4, 8, 128, 1024], P('dp', 'expert'), may hold values from -6 to 6
- doc_lengths: int32 [4, 8], P('dp', 'expert'), may hold values from 128 to 256, as said below
- expert_ids: int32 [4, 8, 256], P('dp', 'expert'), may hold values from 0 to 15
- slot_ids: int32 [4, 8, 256], P('dp', 'expert'), may hold values from 0 to 31, as said below
- gate_prob: float32 [4, 8, 256], P('dp', 'expert'), may hold values from 0.2 to 1
- norm_gain: float32 [1024], replicated, may hold values from 0.5 to 2
- w_in: bfloat16 [16, 1024, 2816], P('expert', None, 'dp'), may hold values from -0.1875 to 0.1875
- w_out_t: bfloat16 [16, 1024, 2816], P('expert', None, 'dp'), may hold values from -0.109375 to 0.109375
- w_value: bfloat16 [1024, 1024], replicated, may hold values from -0.1875 to 0.1875
Outputs:
- enc_mult: bfloat16 [4, 8, 256, 1024], P('dp', 'expert')
Inputs may be any that keep to these rules, and one draw needn't show every extreme that they name: `slot_ids`: within one document no two tokens share an expert and a slot, and every token has a slot; one expert has all 32 slots used in every document. `doc_lengths`: some document has all 256 tokens.
All inputs are finite; a program needn't handle non-finite values.
Results may differ from a plain program's by a relative error of at most 0.0069.
Values may be sent and summed in bfloat16 or wider, within the bound.
A program may use at most 128 MiB of HBM per device.

v0:
```python
import math
import jax
import jax.numpy as jnp
from jax import lax
from jax.sharding import PartitionSpec as P

HEADS = 16
HEAD_DIM = 64


def rescale(pre_act, base_act):
    upper_part = jnp.maximum(jnp.maximum(pre_act, base_act), 0.0)
    lower_part = jnp.maximum(-jnp.minimum(pre_act, base_act), 0.0)
    return upper_part / (upper_part + lower_part + jnp.where(upper_part > 0.0, 0.0, 1.0))


def attend(query_rows, key_rows, mult_rows, length, w_value):
    enc_len = key_rows.shape[0]
    dec_len = query_rows.shape[0]
    queries = query_rows.reshape(dec_len, HEADS, HEAD_DIM)
    keys = key_rows.reshape(enc_len, HEADS, HEAD_DIM)
    mults = mult_rows.reshape(dec_len, HEADS, HEAD_DIM)
    scores = jnp.einsum("qhd,khd->hqk", queries, keys, preferred_element_type=jnp.float32) * (
        1.0 / math.sqrt(HEAD_DIM)
    )
    valid = jnp.arange(enc_len, dtype=jnp.int32) < length
    scores = jnp.where(valid[None, None, :], scores, -jnp.inf)
    top_score = jnp.max(scores, axis=-1, keepdims=True)
    expo = jnp.exp(scores - top_score)
    attn = (expo / jnp.sum(expo, axis=-1, keepdims=True)).astype(jnp.bfloat16)
    value_mult = jnp.einsum("hqk,qhd->khd", attn, mults, preferred_element_type=jnp.float32).astype(
        jnp.bfloat16
    )
    return lax.dot_general(
        value_mult.reshape(enc_len, HEADS * HEAD_DIM),
        w_value,
        (((1,), (1,)), ((), ())),
        preferred_element_type=jnp.float32,
    )


def expert_terms(rows_in, rows_base, rows_mult, part_in, part_out):
    pre_act = jnp.einsum("erd,edf->erf", rows_in, part_in, preferred_element_type=jnp.float32)
    base_act = jnp.einsum("erd,edf->erf", rows_base, part_in, preferred_element_type=jnp.float32)
    hidden_mult = jnp.einsum(
        "erd,edf->erf", rows_mult, part_out, preferred_element_type=jnp.float32
    )
    act_mult = (rescale(pre_act, base_act) * hidden_mult).astype(jnp.bfloat16)
    return jnp.einsum("erf,edf->erd", act_mult, part_in, preferred_element_type=jnp.float32)


def body(
    enc_state,
    baseline,
    enc_keys,
    dec_queries,
    out_mult,
    doc_lengths,
    expert_ids,
    slot_ids,
    gate_prob,
    norm_gain,
    w_in,
    w_out_t,
    w_value,
):
    enc_len = enc_state.shape[2]
    feature_width = enc_state.shape[3]
    local_experts = w_in.shape[0]
    n_experts = local_experts * lax.axis_size("expert")
    capacity = max(2, 2 * enc_len // n_experts)
    tokens = enc_state[0, 0].astype(jnp.float32)
    row_scale = norm_gain * lax.rsqrt(jnp.mean(tokens * tokens, axis=-1, keepdims=True) + 1e-06)
    inputs = (tokens * row_scale).astype(jnp.bfloat16)
    base_inputs = (baseline[0, 0].astype(jnp.float32) * row_scale).astype(jnp.bfloat16)
    flat_slot = expert_ids[0, 0] * capacity + slot_ids[0, 0]
    onehot = (
        flat_slot[None, :] == jnp.arange(n_experts * capacity, dtype=jnp.int32)[:, None]
    ).astype(jnp.bfloat16)

    def dispatch(values):
        placed = jnp.dot(onehot, values, preferred_element_type=jnp.float32).astype(jnp.bfloat16)
        return placed.reshape(n_experts, capacity, feature_width)

    layer_mult = attend(
        dec_queries[0, 0], enc_keys[0, 0], out_mult[0, 0], doc_lengths[0, 0], w_value
    )
    scaled_mult = (gate_prob[0, 0][:, None] * layer_mult).astype(jnp.bfloat16)
    sent_in, sent_base, sent_mult = (
        lax.all_to_all(dispatch(inputs), "expert", split_axis=0, concat_axis=1, tiled=True),
        lax.all_to_all(dispatch(base_inputs), "expert", split_axis=0, concat_axis=1, tiled=True),
        lax.all_to_all(dispatch(scaled_mult), "expert", split_axis=0, concat_axis=1, tiled=True),
    )
    slot_mult = expert_terms(
        sent_in,
        sent_base,
        sent_mult,
        lax.all_gather(w_in, "dp", axis=2, tiled=True),
        lax.all_gather(w_out_t, "dp", axis=2, tiled=True),
    )
    returned = lax.all_to_all(
        slot_mult.astype(jnp.bfloat16), "expert", split_axis=1, concat_axis=0, tiled=True
    )
    per_token = lax.dot_general(
        onehot,
        returned.reshape(n_experts * capacity, feature_width),
        (((0,), (0,)), ((), ())),
        preferred_element_type=jnp.float32,
    )
    result = (layer_mult + row_scale * per_token).astype(jnp.bfloat16)
    return result[None, None]


def solution(mesh):
    in_specs = (
        P("dp", "expert", None, None),
        P("dp", "expert", None, None),
        P("dp", "expert", None, None),
        P("dp", "expert", None, None),
        P("dp", "expert", None, None),
        P("dp", "expert"),
        P("dp", "expert", None),
        P("dp", "expert", None),
        P("dp", "expert", None),
        P(),
        P("expert", None, "dp"),
        P("expert", None, "dp"),
        P(),
    )
    out_specs = P("dp", "expert", None, None)
    return jax.shard_map(body, mesh=mesh, in_specs=in_specs, out_specs=out_specs, check_vma=False)
```

profile of v0, /device:TPU:0, one launch (start us, length us, event | category | flops | bytes accessed | tf_op | source)
XLA Modules:
  0.0 230.6 jit_solution(66276424766294604)
XLA Ops:
  8.3 2.6 %convolution_convert_fusion.1 = bf16[512,1024]{1,0:T(8,128)(2,1)} fusion(bf16[1,1,256,1024]{3,2,1,0:T(8,128)(2,1)} %param.14, f32[256]{0:T(256)S(1)} %add_rsqrt_fusion, f32[1024]{0:T(1024)S(1)} %copy-done.6, s32[256]{0:T(256)S(1)} %bitcast.71), kind=kOutput, calls=%fused_computation.10 | convolution fusion | flops 270139392 | bytes 1579008 | tf_op jit(solution)/shard_map/dot_general | solution.py:82
  10.9 7.3 %all-to-all-start.1 = ((bf16[16,32,1024]{2,1,0:T(8,128)(2,1)}), bf16[16,32,1024]{2,1,0:T(8,128)(2,1)S(1)}, u32[]{:S(2)}, u32[]{:S(2)}) async-start(bf16[16,32,1024]{2,1,0:T(8,128)(2,1)} %bitcast.66), calls=%async_computation.1 | async-start | bytes 2097152 | tf_op jit(solution)/shard_map/all_to_all | solution.py:91
  18.2 2.6 %convolution_convert_fusion.2 = bf16[512,1024]{1,0:T(8,128)(2,1)} fusion(bf16[1,1,256,1024]{3,2,1,0:T(8,128)(2,1)} %param.13, f32[256]{0:T(256)S(1)} %add_rsqrt_fusion, f32[1024]{0:T(1024)S(1)} %copy-done.6, s32[256]{0:T(256)S(1)} %bitcast.72), kind=kOutput, calls=%fused_computation.11 | convolution fusion | flops 270139392 | bytes 1579008 | tf_op jit(solution)/shard_map/dot_general | solution.py:82
  20.8 23.1 %all-to-all-done.1 = bf16[16,32,1024]{2,1,0:T(8,128)(2,1)S(1)} async-done(((bf16[16,32,1024]{2,1,0:T(8,128)(2,1)}), bf16[16,32,1024]{2,1,0:T(8,128)(2,1)S(1)}, u32[]{:S(2)}, u32[]{:S(2)}) %all-to-all-start.1) | async-done | bytes 1048608 | tf_op jit(solution)/shard_map/all_to_all | solution.py:91
  44.0 4.2 %all-to-all-start = ((bf16[16,32,1024]{2,1,0:T(8,128)(2,1)}), bf16[16,32,1024]{2,1,0:T(8,128)(2,1)}, u32[]{:S(2)}, u32[]{:S(2)}) async-start(bf16[16,32,1024]{2,1,0:T(8,128)(2,1)} %bitcast.62), calls=%async_computation | async-start | bytes 2097152 | tf_op jit(solution)/shard_map/all_to_all | solution.py:90
  49.7 1.1 copy.41
  50.8 2.0 copy.40
  52.9 3.2 %fusion.28 = (f32[16,128]{1,0:T(8,128)S(1)}, f32[16,128,256]{2,1,0:T(8,128)}) fusion(pred[256]{0:T(512)(128)(4,1)S(1)} %iota_compare_fusion.5, bf16[128,16,64]{0,2,1:T(8,128)(2,1)} %bitcast.70, bf16[256,16,64]{0,2,1:T(8,128)(2,1)} %bitcast.68), kind=kOutput, calls=%fused_computation.43 | convolution fusion | flops 69206272 | bytes 2892032 | tf_op jit(solution)/shard_map/sub | solution.py:29
  56.0 2.2 convolution_convert_fusion.4
  59.1 1.5 convolution_convert_fusion
  60.6 13.2 %all-to-all-done = bf16[16,32,1024]{2,1,0:T(8,128)(2,1)} async-done(((bf16[16,32,1024]{2,1,0:T(8,128)(2,1)}), bf16[16,32,1024]{2,1,0:T(8,128)(2,1)}, u32[]{:S(2)}, u32[]{:S(2)}) %all-to-all-start) | async-done | bytes 1048608 | tf_op jit(solution)/shard_map/all_to_all | solution.py:90
  73.8 3.7 %all-to-all-start.2 = ((bf16[16,32,1024]{2,1,0:T(8,128)(2,1)}), bf16[16,32,1024]{2,1,0:T(8,128)(2,1)S(1)}, u32[]{:S(2)}, u32[]{:S(2)}) async-start(bf16[16,32,1024]{2,1,0:T(8,128)(2,1)} %bitcast.19), calls=%async_computation.2 | async-start | bytes 2097152 | tf_op jit(solution)/shard_map/all_to_all | solution.py:92
  77.5 1.3 copy.43
  78.8 2.4 %copy.42 = bf16[8,2,32,1024]{3,2,0,1:T(8,128)(2,1)} copy(bf16[8,2,32,1024]{3,2,1,0:T(8,128)(2,1)} %bitcast.10) | data formatting | bytes 2097152 | tf_op jit(solution)/shard_map/all_to_all | solution.py:90
  81.3 22.0 %all-to-all-done.2 = bf16[16,32,1024]{2,1,0:T(8,128)(2,1)S(1)} async-done(((bf16[16,32,1024]{2,1,0:T(8,128)(2,1)}), bf16[16,32,1024]{2,1,0:T(8,128)(2,1)S(1)}, u32[]{:S(2)}, u32[]{:S(2)}) %all-to-all-start.2) | async-done | bytes 1048608 | tf_op jit(solution)/shard_map/all_to_all | solution.py:92
  103.2 1.1 copy.44
  104.3 10.3 %fusion.30 = f32[2,256,2816]{2,1,0:T(8,128)} fusion(bf16[2,256,1024]{2,1,0:T(8,128)(2,1)} %bitcast.65, bf16[2,1024,2816]{1,2,0:T(8,128)(2,1)} %all-gather.3.cloned.1.call-done), kind=kOutput, calls=%fused_computation.45 | convolution fusion | flops 2952790016 | bytes 18350080 | tf_op jit(solution)/shard_map/erd,edf->erf/dot_general | solution.py:43
  114.6 13.8 %fusion.31 = f32[2,256,2816]{2,1,0:T(8,128)} fusion(bf16[2,256,1024]{2,1,0:T(8,128)(2,1)S(1)} %bitcast.63, bf16[2,1024,2816]{1,2,0:T(8,128)(2,1)} %all-gather.3.cloned.1.call-done), kind=kOutput, calls=%fused_computation.46 | convolution fusion | flops 2952790016 | bytes 18350080 | tf_op jit(solution)/shard_map/erd,edf->erf/dot_general | solution.py:44
  128.4 37.1 %all-gather.5.cloned.1.call-done = bf16[2,1024,2816]{1,2,0:T(8,128)(2,1)} async-done(((bf16[2,1024,704]{1,2,0:T(8,128)(2,1)}), bf16[2,1024,2816]{1,2,0:T(8,128)(2,1)}) %all-gather.5.cloned.1.call-update) | async-done | bytes 11534352 | tf_op jit(solution)/shard_map/all_gather | solution.py:99
  165.5 15.6 %multiply_convert_fusion = bf16[2,256,2816]{2,1,0:T(8,128)(2,1)} fusion(f32[2,256,2816]{2,1,0:T(8,128)} %fusion.30, f32[2,256,2816]{2,1,0:T(8,128)} %fusion.31, bf16[2,256,1024]{2,1,0:T(8,128)(2,1)S(1)} %bitcast.64, bf16[2,1024,2816]{1,2,0:T(8,128)(2,1)} %all-gather.5.cloned.1.call-done), kind=kOutput, calls=%fused_computation.1 | convolution fusion | flops 2970091520 | bytes 27000832 | tf_op jit(solution)/shard_map/erd,edf->erf/dot_general | solution.py:45
  181.1 8.4 %convolution_convert_fusion.3 = bf16[2,256,1024]{2,1,0:T(8,128)(2,1)S(1)} fusion(bf16[2,256,2816]{2,1,0:T(8,128)(2,1)} %multiply_convert_fusion, bf16[2,1024,2816]{1,2,0:T(8,128)(2,1)} %all-gather.3.cloned.1.call-done), kind=kOutput, calls=%fused_computation.12 | convolution fusion | flops 2953314304 | bytes 15466496 | tf_op jit(solution)/shard_map/erf,edf->erd/dot_general | solution.py:49
  189.5 1.1 copy.45
  190.6 31.4 %all_to_all.69 = bf16[2,256,1024]{2,0,1:T(2,128)(2,1)S(1)} all-to-all(bf16[2,256,1024]{2,0,1:T(2,128)(2,1)S(1)} %copy.45), channel_id=1, replica_groups=mesh['expert'=8,'dp'=4] {'expert'}, dimensions={1} | all-to-all | bytes 2097152 | tf_op jit(solution)/shard_map/all_to_all | solution.py:101
  222.4 1.3 fusion.4
  (33 shorter events, 3.6 us)
Async XLA Ops:
  6.5 51.7 %copy-start = (bf16[1024,1024]{1,0:T(8,128)(2,1)S(1)}, bf16[1024,1024]{1,0:T(8,128)(2,1)}, u32[]{:S(2)}) copy-start(bf16[1024,1024]{1,0:T(8,128)(2,1)} %param.25) | copy-start | bytes 6291460
  6.5 1.5 copy-start.4
  6.5 1.7 copy-start.8
  6.5 1.7 copy-start.9
  6.5 1.7 copy-start.6
  6.5 97.8 %all-gather.3.cloned.1.call-start = ((), (), s32[]{:S(2)}) async-start(), calls=%async_computation.4 | async-start | bytes 14417920 | tf_op jit(solution)/shard_map/all_gather | solution.py:98
  7.3 41.6 %copy-start.5 = (bf16[1,1,128,1024]{3,2,1,0:T(8,128)(2,1)S(1)}, bf16[1,1,128,1024]{3,2,1,0:T(8,128)(2,1)}, u32[]{:S(2)}) copy-start(bf16[1,1,128,1024]{3,2,1,0:T(8,128)(2,1)} %param.16) | copy-start | bytes 786436
  7.3 158.2 %all-gather.5.cloned.1.call-start = ((), (), s32[]{:S(2)}) async-start(), calls=%async_computation.5 | async-start | bytes 14417920 | tf_op jit(solution)/shard_map/all_gather | solution.py:99
  10.9 33.0 %all-to-all-start.1 = ((bf16[16,32,1024]{2,1,0:T(8,128)(2,1)}), bf16[16,32,1024]{2,1,0:T(8,128)(2,1)S(1)}, u32[]{:S(2)}, u32[]{:S(2)}) async-start(bf16[16,32,1024]{2,1,0:T(8,128)(2,1)} %bitcast.66), calls=%async_computation.1 | async-start | bytes 2097152 | tf_op jit(solution)/shard_map/all_to_all | solution.py:91
  44.0 14.3 %copy-start.2 = (bf16[16,32,1024]{2,1,0:T(8,128)(2,1)}, bf16[16,32,1024]{2,1,0:T(8,128)(2,1)S(1)}, u32[]{:S(2)}) copy-start(bf16[16,32,1024]{2,1,0:T(8,128)(2,1)S(1)} %all-to-all-done.1) | copy-start | bytes 3145732
  44.0 29.8 %all-to-all-start = ((bf16[16,32,1024]{2,1,0:T(8,128)(2,1)}), bf16[16,32,1024]{2,1,0:T(8,128)(2,1)}, u32[]{:S(2)}, u32[]{:S(2)}) async-start(bf16[16,32,1024]{2,1,0:T(8,128)(2,1)} %bitcast.62), calls=%async_computation | async-start | bytes 2097152 | tf_op jit(solution)/shard_map/all_to_all | solution.py:90
  56.0 3.0 %copy-start.7 = (f32[1,1,256]{2,1,0:T(1,128)S(1)}, f32[1,1,256]{2,1,0:T(1,128)}, u32[]{:S(2)}) copy-start(f32[1,1,256]{2,1,0:T(1,128)} %param.21) | copy-start | bytes 3076
  73.8 29.5 %all-to-all-start.2 = ((bf16[16,32,1024]{2,1,0:T(8,128)(2,1)}), bf16[16,32,1024]{2,1,0:T(8,128)(2,1)S(1)}, u32[]{:S(2)}, u32[]{:S(2)}) async-start(bf16[16,32,1024]{2,1,0:T(8,128)(2,1)} %bitcast.19), calls=%async_computation.2 | async-start | bytes 2097152 | tf_op jit(solution)/shard_map/all_to_all | solution.py:92
  114.6 50.9 %copy-start.3 = (bf16[2,8,32,1024]{3,2,1,0:T(8,128)(2,1)S(1)}, bf16[2,8,32,1024]{3,2,1,0:T(8,128)(2,1)}, u32[]{:S(2)}) copy-start(bf16[2,8,32,1024]{3,2,1,0:T(8,128)(2,1)} %copy.44) | copy-start | bytes 3145732
  181.1 42.6 %copy-start.1 = (bf16[1024,1024]{1,0:T(8,128)(2,1)S(1)}, bf16[1024,1024]{1,0:T(8,128)(2,1)}, u32[]{:S(2)}) copy-start(bf16[1024,1024]{1,0:T(8,128)(2,1)} %param.25) | copy-start | bytes 6291460
Sparse Core Ops, SparseCore 0:
  8.9 78.8 all-gather.2
  89.4 76.1 all-gather.4
where the time goes:
time: 231 us
  waiting for transfers between devices  96.8 us (42%)
  matrix products  62.3 us (27%)
  blocking collectives  31.4 us (14%)
  starting transfers between devices  15.3 us (7%)
  between operations  14.2 us (6%)
  local copies, waits for them, and re-layouts  10.3 us (4%)
    all_gather x1, waiting for transfers between devices, body(): lax.all_gather(w_out_t, 'dp', axis=2, tiled=True)  37.1 us
    all_to_all x1, blocking collectives, body(): lax.all_to_all(slot_mult.astype(jnp.bfloat16), 'expert', split_axis=1, co...  31.4 us
    all_to_all x1, waiting for transfers between devices, body(): lax.all_to_all(dispatch(base_inputs), 'expert', split_axis=0, concat_axis...  23.1 us
    all_to_all x1, waiting for transfers between devices, body(): lax.all_to_all(dispatch(scaled_mult), 'expert', split_axis=0, concat_axis...  22 us
    dot_general x1, matrix products, expert_terms(): jnp.einsum('erd,edf->erf', rows_mult, part_out, preferred_element_type=jn...  15.6 us
    dot_general x1, matrix products, expert_terms(): jnp.einsum('erd,edf->erf', rows_base, part_in, preferred_element_type=jnp...  13.8 us
    all_to_all x1, waiting for transfers between devices, body(): lax.all_to_all(dispatch(inputs), 'expert', split_axis=0, concat_axis=1, t...  13.2 us
    dot_general x1, matrix products, expert_terms(): jnp.einsum('erd,edf->erf', rows_in, part_in, preferred_element_type=jnp.f...  10.3 us
  transfers between devices with their start and end apart: 5, of which 4 were waited for; matrix products, arithmetic and copies ran while one was open for 20% of the time, Pallas kernels for 0%

commit v1 on v0

--- a/solution.py
+++ b/solution.py
@@ -6,6 +6,12 @@
 
 HEADS = 16
 HEAD_DIM = 64
+
+
+def stacked_exchange(x, name, split, join):
+    cells = jnp.split(x, lax.axis_size(name), axis=split)
+    arrived = lax.all_to_all(jnp.stack(cells), name, 0, 0)
+    return jnp.concatenate(arrived, axis=join)
 
 
 def rescale(pre_act, base_act):
@@ -88,7 +94,7 @@
     scaled_mult = (gate_prob[0, 0][:, None] * layer_mult).astype(jnp.bfloat16)
     sent_in, sent_base, sent_mult = (
         lax.all_to_all(dispatch(inputs), "expert", split_axis=0, concat_axis=1, tiled=True),
-        lax.all_to_all(dispatch(base_inputs), "expert", split_axis=0, concat_axis=1, tiled=True),
+        stacked_exchange(dispatch(base_inputs), "expert", 0, 1),
         lax.all_to_all(dispatch(scaled_mult), "expert", split_axis=0, concat_axis=1, tiled=True),
     )
     slot_mult = expert_terms(

time: 231 us -> 231 us (level)
  local copies, waits for them, and re-layouts: 10.3 us -> 15.6 us
  waiting for transfers between devices: 96.8 us -> 92.5 us
    unnamed x23 -> x30, local copies, waits for them, and re-layouts: 4.04 us -> 8.65 us
    all_gather x1, waiting for transfers between devices: 37.1 us -> 32.6 us  [body(): lax.all_gather(w_out_t, 'dp', axis=2, tiled=True)]
  transfers between devices with their start and end apart: 5 -> 5, of which waited for: 4 -> 4; matrix products, arithmetic and copies ran while one was open for 20% -> 22% of each run, Pallas kernels for 0% -> 0%
where the time goes in v1:
time: 231 us
  waiting for transfers between devices  92.5 us (40%)
  matrix products  61.3 us (27%)
  blocking collectives  31.4 us (14%)
  local copies, waits for them, and re-layouts  15.6 us (7%)
  starting transfers between devices  15.3 us (7%)
  between operations  14.2 us (6%)
    all_gather x1, waiting for transfers between devices, body(): lax.all_gather(w_out_t, 'dp', axis=2, tiled=True)  32.6 us
    all_to_all x1, blocking collectives, body(): lax.all_to_all(slot_mult.astype(jnp.bfloat16), 'expert', split_axis=1, co...  31.4 us
    all_to_all x1, waiting for transfers between devices, stacked_exchange(): arrived = lax.all_to_all(jnp.stack(cells), name, 0, 0)  23.2 us
    all_to_all x1, waiting for transfers between devices, body(): lax.all_to_all(dispatch(scaled_mult), 'expert', split_axis=0, concat_axis...  22.1 us
    dot_general x1, matrix products, expert_terms(): jnp.einsum('erd,edf->erf', rows_mult, part_out, preferred_element_type=jn...  15.6 us
    dot_general x1, matrix products, expert_terms(): jnp.einsum('erd,edf->erf', rows_base, part_in, preferred_element_type=jnp...  13.7 us
    all_to_all x1, waiting for transfers between devices, body(): lax.all_to_all(dispatch(inputs), 'expert', split_axis=0, concat_axis=1, t...  13.3 us
    dot_general x1, matrix products, expert_terms(): jnp.einsum('erd,edf->erf', rows_in, part_in, preferred_element_type=jnp.f...  10.4 us
  transfers between devices with their start and end apart: 5, of which 4 were waited for; matrix products, arithmetic and copies ran while one was open for 22% of the time, Pallas kernels for 0%

profile of v1, /device:TPU:0, one launch (start us, length us, event | category | flops | bytes accessed | tf_op | source)
XLA Modules:
  0.0 230.6 jit_solution(638680258245271635)
XLA Ops:
  8.3 1.6 convolution_convert_fusion.1
  15.3 7.3 %all-to-all-start.1 = ((bf16[8,2,32,1024]{3,2,1,0:T(8,128)(2,1)}), bf16[8,2,32,1024]{3,2,1,0:T(8,128)(2,1)S(1)}, u32[]{:S(2)}, u32[]{:S(2)}) async-start(bf16[8,2,32,1024]{3,2,1,0:T(8,128)(2,1)} %constant_dynamic-update-slice_fusion), calls=%async_computation.1 | async-start | bytes 2097152 | tf_op jit(solution)/shard_map/all_to_all | solution.py:13
  22.6 2.6 %convolution_convert_fusion.2 = bf16[512,1024]{1,0:T(8,128)(2,1)} fusion(bf16[1,1,256,1024]{3,2,1,0:T(8,128)(2,1)} %param.13, f32[256]{0:T(256)S(1)} %add_rsqrt_fusion, f32[1024]{0:T(1024)S(1)} %copy-done.6, s32[256]{0:T(256)S(1)} %bitcast.84), kind=kOutput, calls=%fused_computation.11 | convolution fusion | flops 270139392 | bytes 1579008 | tf_op jit(solution)/shard_map/dot_general | solution.py:88
  25.2 23.2 %all-to-all-done.1 = bf16[8,2,32,1024]{3,2,1,0:T(8,128)(2,1)S(1)} async-done(((bf16[8,2,32,1024]{3,2,1,0:T(8,128)(2,1)}), bf16[8,2,32,1024]{3,2,1,0:T(8,128)(2,1)S(1)}, u32[]{:S(2)}, u32[]{:S(2)}) %all-to-all-start.1) | async-done | bytes 1048608 | tf_op jit(solution)/shard_map/all_to_all | solution.py:13
  48.4 4.2 %all-to-all-start = ((bf16[16,32,1024]{2,1,0:T(8,128)(2,1)}), bf16[16,32,1024]{2,1,0:T(8,128)(2,1)}, u32[]{:S(2)}, u32[]{:S(2)}) async-start(bf16[16,32,1024]{2,1,0:T(8,128)(2,1)} %bitcast.67), calls=%async_computation | async-start | bytes 2097152 | tf_op jit(solution)/shard_map/all_to_all | solution.py:96
  54.1 1.1 copy.41
  55.2 2.0 copy.40
  57.3 3.2 %fusion.29 = (f32[16,128]{1,0:T(8,128)S(1)}, f32[16,128,256]{2,1,0:T(8,128)}) fusion(pred[256]{0:T(512)(128)(4,1)S(1)} %iota_compare_fusion.5, bf16[128,16,64]{0,2,1:T(8,128)(2,1)} %bitcast.82, bf16[256,16,64]{0,2,1:T(8,128)(2,1)} %bitcast.80), kind=kOutput, calls=%fused_computation.52 | convolution fusion | flops 69206272 | bytes 2892032 | tf_op jit(solution)/shard_map/sub | solution.py:35
  60.4 2.2 convolution_convert_fusion.4
  63.4 1.5 convolution_convert_fusion
  64.9 13.3 %all-to-all-done = bf16[16,32,1024]{2,1,0:T(8,128)(2,1)} async-done(((bf16[16,32,1024]{2,1,0:T(8,128)(2,1)}), bf16[16,32,1024]{2,1,0:T(8,128)(2,1)}, u32[]{:S(2)}, u32[]{:S(2)}) %all-to-all-start) | async-done | bytes 1048608 | tf_op jit(solution)/shard_map/all_to_all | solution.py:96
  78.2 3.7 %all-to-all-start.2 = ((bf16[16,32,1024]{2,1,0:T(8,128)(2,1)}), bf16[16,32,1024]{2,1,0:T(8,128)(2,1)S(1)}, u32[]{:S(2)}, u32[]{:S(2)}) async-start(bf16[16,32,1024]{2,1,0:T(8,128)(2,1)} %bitcast.25), calls=%async_computation.2 | async-start | bytes 2097152 | tf_op jit(solution)/shard_map/all_to_all | solution.py:98
  81.9 1.3 copy.43
  83.3 2.3 %copy.42 = bf16[8,2,32,1024]{3,2,0,1:T(8,128)(2,1)} copy(bf16[8,2,32,1024]{3,2,1,0:T(8,128)(2,1)} %bitcast.10) | data formatting | bytes 2097152 | tf_op jit(solution)/shard_map/all_to_all | solution.py:96
  85.6 22.1 %all-to-all-done.2 = bf16[16,32,1024]{2,1,0:T(8,128)(2,1)S(1)} async-done(((bf16[16,32,1024]{2,1,0:T(8,128)(2,1)}), bf16[16,32,1024]{2,1,0:T(8,128)(2,1)S(1)}, u32[]{:S(2)}, u32[]{:S(2)}) %all-to-all-start.2) | async-done | bytes 1048608 | tf_op jit(solution)/shard_map/all_to_all | solution.py:98
  107.7 1.1 copy.44
  108.7 10.4 %fusion.31 = f32[2,256,2816]{2,1,0:T(8,128)} fusion(bf16[2,256,1024]{2,1,0:T(8,128)(2,1)} %bitcast.70, bf16[2,1024,2816]{1,2,0:T(8,128)(2,1)} %all-gather.3.cloned.1.call-done), kind=kOutput, calls=%fused_computation.54 | convolution fusion | flops 2952790016 | bytes 18350080 | tf_op jit(solution)/shard_map/erd,edf->erf/dot_general | solution.py:49
  119.1 13.7 %fusion.32 = f32[2,256,2816]{2,1,0:T(8,128)} fusion(bf16[2,256,1024]{2,1,0:T(8,128)(2,1)S(1)} %bitcast.68, bf16[2,1024,2816]{1,2,0:T(8,128)(2,1)} %all-gather.3.cloned.1.call-done), kind=kOutput, calls=%fused_computation.55 | convolution fusion | flops 2952790016 | bytes 18350080 | tf_op jit(solution)/shard_map/erd,edf->erf/dot_general | solution.py:50
  132.9 32.6 %all-gather.5.cloned.1.call-done = bf16[2,1024,2816]{1,2,0:T(8,128)(2,1)} async-done(((bf16[2,1024,704]{1,2,0:T(8,128)(2,1)}), bf16[2,1024,2816]{1,2,0:T(8,128)(2,1)}) %all-gather.5.cloned.1.call-update) | async-done | bytes 11534352 | tf_op jit(solution)/shard_map/all_gather | solution.py:105
  165.5 15.6 %multiply_convert_fusion = bf16[2,256,2816]{2,1,0:T(8,128)(2,1)} fusion(f32[2,256,2816]{2,1,0:T(8,128)} %fusion.31, f32[2,256,2816]{2,1,0:T(8,128)} %fusion.32, bf16[2,256,1024]{2,1,0:T(8,128)(2,1)S(1)} %bitcast.69, bf16[2,1024,2816]{1,2,0:T(8,128)(2,1)} %all-gather.5.cloned.1.call-done), kind=kOutput, calls=%fused_computation.1 | convolution fusion | flops 2970091520 | bytes 27000832 | tf_op jit(solution)/shard_map/erd,edf->erf/dot_general | solution.py:51
  181.1 8.4 %convolution_convert_fusion.3 = bf16[2,256,1024]{2,1,0:T(8,128)(2,1)S(1)} fusion(bf16[2,256,2816]{2,1,0:T(8,128)(2,1)} %multiply_convert_fusion, bf16[2,1024,2816]{1,2,0:T(8,128)(2,1)} %all-gather.3.cloned.1.call-done), kind=kOutput, calls=%fused_computation.12 | convolution fusion | flops 2953314304 | bytes 15466496 | tf_op jit(solution)/shard_map/erf,edf->erd/dot_general | solution.py:55
  189.6 1.1 copy.45
  190.7 31.4 %all_to_all.56 = bf16[2,256,1024]{2,0,1:T(2,128)(2,1)S(1)} all-to-all(bf16[2,256,1024]{2,0,1:T(2,128)(2,1)S(1)} %copy.45), channel_id=1, replica_groups=mesh['expert'=8,'dp'=4] {'expert'}, dimensions={1} | all-to-all | bytes 2097152 | tf_op jit(solution)/shard_map/all_to_all | solution.py:107
  222.5 1.3 fusion.4
  (42 shorter events, 9.0 us)
Async XLA Ops:
  6.5 56.1 %copy-start = (bf16[1024,1024]{1,0:T(8,128)(2,1)S(1)}, bf16[1024,1024]{1,0:T(8,128)(2,1)}, u32[]{:S(2)}) copy-start(bf16[1024,1024]{1,0:T(8,128)(2,1)} %param.25) | copy-start | bytes 6291460
  6.5 1.5 copy-start.4
  6.5 1.7 copy-start.8
  6.5 1.7 copy-start.9
  6.5 1.7 copy-start.6
  6.5 102.2 %all-gather.3.cloned.1.call-start = ((), (), s32[]{:S(2)}) async-start(), calls=%async_computation.4 | async-start | bytes 14417920 | tf_op jit(solution)/shard_map/all_gather | solution.py:104
  7.3 158.2 %all-gather.5.cloned.1.call-start = ((), (), s32[]{:S(2)}) async-start(), calls=%async_computation.5 | async-start | bytes 14417920 | tf_op jit(solution)/shard_map/all_gather | solution.py:105
  8.3 45.0 %copy-start.5 = (bf16[1,1,128,1024]{3,2,1,0:T(8,128)(2,1)S(1)}, bf16[1,1,128,1024]{3,2,1,0:T(8,128)(2,1)}, u32[]{:S(2)}) copy-start(bf16[1,1,128,1024]{3,2,1,0:T(8,128)(2,1)} %param.16) | copy-start | bytes 786436
  15.3 33.0 %all-to-all-start.1 = ((bf16[8,2,32,1024]{3,2,1,0:T(8,128)(2,1)}), bf16[8,2,32,1024]{3,2,1,0:T(8,128)(2,1)S(1)}, u32[]{:S(2)}, u32[]{:S(2)}) async-start(bf16[8,2,32,1024]{3,2,1,0:T(8,128)(2,1)} %constant_dynamic-update-slice_fusion), calls=%async_computation.1 | async-start | bytes 2097152 | tf_op jit(solution)/shard_map/all_to_all | solution.py:13
  48.4 14.2 %copy-start.2 = (bf16[8,2,32,1024]{3,2,1,0:T(8,128)(2,1)}, bf16[8,2,32,1024]{3,2,1,0:T(8,128)(2,1)S(1)}, u32[]{:S(2)}) copy-start(bf16[8,2,32,1024]{3,2,1,0:T(8,128)(2,1)S(1)} %all-to-all-done.1) | copy-start | bytes 3145732
  48.4 29.8 %all-to-all-start = ((bf16[16,32,1024]{2,1,0:T(8,128)(2,1)}), bf16[16,32,1024]{2,1,0:T(8,128)(2,1)}, u32[]{:S(2)}, u32[]{:S(2)}) async-start(bf16[16,32,1024]{2,1,0:T(8,128)(2,1)} %bitcast.67), calls=%async_computation | async-start | bytes 2097152 | tf_op jit(solution)/shard_map/all_to_all | solution.py:96
  60.4 3.0 %copy-start.7 = (f32[1,1,256]{2,1,0:T(1,128)S(1)}, f32[1,1,256]{2,1,0:T(1,128)}, u32[]{:S(2)}) copy-start(f32[1,1,256]{2,1,0:T(1,128)} %param.21) | copy-start | bytes 3076
  78.2 29.5 %all-to-all-start.2 = ((bf16[16,32,1024]{2,1,0:T(8,128)(2,1)}), bf16[16,32,1024]{2,1,0:T(8,128)(2,1)S(1)}, u32[]{:S(2)}, u32[]{:S(2)}) async-start(bf16[16,32,1024]{2,1,0:T(8,128)(2,1)} %bitcast.25), calls=%async_computation.2 | async-start | bytes 2097152 | tf_op jit(solution)/shard_map/all_to_all | solution.py:98
  119.1 46.4 %copy-start.3 = (bf16[2,8,32,1024]{3,2,1,0:T(8,128)(2,1)S(1)}, bf16[2,8,32,1024]{3,2,1,0:T(8,128)(2,1)}, u32[]{:S(2)}) copy-start(bf16[2,8,32,1024]{3,2,1,0:T(8,128)(2,1)} %copy.44) | copy-start | bytes 3145732
  181.1 42.6 %copy-start.1 = (bf16[1024,1024]{1,0:T(8,128)(2,1)S(1)}, bf16[1024,1024]{1,0:T(8,128)(2,1)}, u32[]{:S(2)}) copy-start(bf16[1024,1024]{1,0:T(8,128)(2,1)} %param.25) | copy-start | bytes 6291460
Sparse Core Ops, SparseCore 0:
  8.9 78.8 all-gather.2
  89.4 76.1 all-gather.4
